TPU v7x, 32 devices: a whole 2x2x4 slice. The times are simulated.
32 devices in a mesh: blk: 16 (over z, y, core), rep: 2 (over x).
Axes of the slice: x: 2, y: 2, z: 4, core: 2. Of those that a mesh axis runs over, the one named last changes fastest.
Arguments:
- raw_integrals: float32 [16, 1024, 512], P(None, 'blk'), may hold values from -0.6 to 0.6
- virtual_coeffs: float32 [512, 256], P(None, 'rep'), may hold values from -0.25 to 0.25
- metric_root: float32 [1024, 1024], P(None, 'rep'), may hold values from -1 to 3, as said below
- occ_energies: float32 [16], P('blk'), may hold values from -2 to -0.5
- virt_energies: float32 [256], replicated, may hold values from 0.2 to 3
Outputs:
- gamma: float32 [16, 256, 1024], P('blk', None, 'rep')
Inputs may be any that keep to these rules, and one draw needn't show every extreme that they name: metric_root is exactly symmetric.
All inputs are finite; a program needn't handle non-finite values.
Results may differ from a plain program's by a relative error of at most 0.0001.
Values sent between devices are 32-bit elements; how exact they have to be, the bound alone decides.
No kernel may reach another device: no remote copies, remote signals or barrier semaphores. Data moves between devices by JAX's collectives and lax.ppermute only.
A program may use at most 64 MiB of HBM per device.

v0:
```python
import jax
import jax.numpy as jnp
from jax import lax
from jax.sharding import PartitionSpec as P

TURNS = 2


def from_behind(x, axis, by):
    count = lax.axis_size(axis)
    return lax.ppermute(x, axis, [(i, (i + by) % count) for i in range(count)])


def pair_terms(own_rows, own_eps, other_rows, other_eps, virt_energies, gradient):
    highest = lax.Precision.HIGHEST
    coulomb = jnp.einsum("xaq,ybq->xyab", own_rows, other_rows, precision=highest)
    spread = virt_energies[:, None] + virt_energies[None, :]
    denominator = spread[None, None] - own_eps[:, None, None, None] - other_eps[None, :, None, None]
    amplitude = (2.0 * coulomb - jnp.swapaxes(coulomb, 2, 3)) / denominator
    return gradient + jnp.einsum("xyab,ybq->xaq", amplitude, other_rows, precision=highest)


def per_device(raw_integrals, virtual_coeffs, metric_root, occ_energies, virt_energies):
    highest = lax.Precision.HIGHEST
    halfway = jnp.einsum("ipm,ma->ipa", raw_integrals, virtual_coeffs, precision=highest)
    regrouped = lax.all_to_all(halfway, "blk", split_axis=0, concat_axis=1, tiled=True)
    complete = lax.all_gather(regrouped, "rep", axis=2, tiled=True)
    fitted_part = jnp.einsum("xpa,pq->xaq", complete, metric_root, precision=highest)
    fitted = lax.all_gather(fitted_part, "rep", axis=2, tiled=True)
    replica = lax.axis_index("rep")
    replicas = lax.axis_size("rep")
    turns = TURNS
    turn_unit = 1
    travel_rows = fitted
    travel_eps = occ_energies
    for bit_index in range((replicas - 1).bit_length()):
        shifted_rows, shifted_eps = from_behind(
            (travel_rows, travel_eps), "blk", (1 << bit_index) * turns
        )
        chosen = replica >> bit_index & 1 == 1
        travel_rows = jnp.where(chosen, shifted_rows, travel_rows)
        travel_eps = jnp.where(chosen, shifted_eps, travel_eps)
    gradient = jnp.zeros(fitted.shape, jnp.float32)

    def advance(turn_index, state_now):
        other_rows, other_eps, total = state_now
        total = pair_terms(fitted, occ_energies, other_rows, other_eps, virt_energies, total)
        other_rows, other_eps = from_behind((other_rows, other_eps), "blk", turn_unit)
        return (other_rows, other_eps, total)

    travel_rows, travel_eps, gradient = lax.fori_loop(
        0, turns - 1, advance, (travel_rows, travel_eps, gradient)
    )
    gradient = pair_terms(fitted, occ_energies, travel_rows, travel_eps, virt_energies, gradient)
    return lax.psum_scatter(gradient, "rep", scatter_dimension=2, tiled=True)


def solution(mesh):
    return jax.shard_map(
        per_device,
        mesh=mesh,
        in_specs=(P(None, "blk", None), P(None, "rep"), P(None, "rep"), P("blk"), P()),
        out_specs=P("blk", None, "rep"),
        check_vma=False,
    )
```

profile of v0, /device:TPU:0, one launch (start us, length us, event | category | flops | bytes accessed | tf_op | source)
XLA Modules:
  0.0 165.9 jit_solution(520824804438171857)
XLA Ops:
  6.5 0.0 copy-start
  6.5 0.0 all-gather.4.cloned.1.call-start
  6.5 1.6 copy-done
  8.1 2.7 %fusion.18 = f32[16,64,128]{2,1,0:T(8,128)S(1)} fusion(f32[16,64,512]{2,1,0:T(8,128)S(1)} %copy-done, f32[512,128]{1,0:T(8,128)} %param.6), kind=kOutput, calls=%fused_computation.20 | convolution fusion | flops 805306368 | bytes 2883584 | tf_op jit(solution)/shard_map/ipm,ma->ipa/dot_general | solution.py:25
  10.9 21.6 %all_to_all.12 = f32[16,64,128]{2,1,0:T(8,128)} all-to-all(f32[16,64,128]{2,1,0:T(8,128)S(1)} %fusion.18), channel_id=1, replica_groups=mesh['blk'=16,'rep'=2] {'blk'}, dimensions={0} | all-to-all | bytes 1048576 | tf_op jit(solution)/shard_map/all_to_all | solution.py:26
  32.5 0.0 all-gather.4.cloned.1.call-update
  32.5 0.0 all-gather.6.cloned.1.call-start
  32.5 20.9 %all-gather.4.cloned.1.call-done = f32[1,1024,256]{2,1,0:T(8,128)} async-done(((f32[1,1024,128]{2,1,0:T(8,128)}), f32[1,1024,256]{2,1,0:T(8,128)}) %all-gather.4.cloned.1.call-update) | async-done | bytes 1048592 | tf_op jit(solution)/shard_map/all_gather | solution.py:27
  53.4 4.6 %fusion.8 = f32[256,512]{1,0:T(8,128)} fusion(f32[1024,512]{1,0:T(8,128)} %param.7, f32[1,1024,256]{2,1,0:T(8,128)} %all-gather.4.cloned.1.call-done), kind=kOutput, calls=%fused_computation.9 | convolution fusion | flops 1610612736 | bytes 3670016 | tf_op jit(solution)/shard_map/xpa,pq->xaq/dot_general | solution.py:28
  58.0 0.0 all-gather.6.cloned.1.call-update
  58.1 0.0 reduce-scatter.2.cloned.1.call-start
  58.1 21.4 %all-gather.6.cloned.1.call-done = f32[256,1024]{1,0:T(8,128)} async-done(((f32[256,512]{1,0:T(8,128)}), f32[256,1024]{1,0:T(8,128)}) %all-gather.6.cloned.1.call-update) | async-done | bytes 1048592 | tf_op jit(solution)/shard_map/all_gather | solution.py:29
  79.5 0.0 copy-start.1
  79.5 1.5 collective-permute-start
  81.0 26.3 %collective-permute-done = f32[1,256,1024]{2,1,0:T(8,128)} collective-permute-done((f32[1,256,1024]{2,1,0:T(8,128)}, f32[1,256,1024]{2,1,0:T(8,128)}, u32[]{:S(2)}, u32[]{:S(2)}) %collective-permute-start) | collective-permute-done | bytes 1048608 | tf_op jit(solution)/shard_map/ppermute | solution.py:11
  107.3 2.4 %broadcast_select_fusion = f32[1,256,1024]{2,1,0:T(8,128)} fusion(f32[1,256,1024]{2,1,0:T(8,128)} %collective-permute-done, pred[]{:T(512)} %eq.3, f32[256,1024]{1,0:T(8,128)} %all-gather.6.cloned.1.call-done), kind=kLoop, calls=%fused_computation.11 | loop fusion | flops 262144 | bytes 3145729 | tf_op jit(solution)/shard_map/jit(_where)/select_n | solution.py:41
  109.7 0.0 collective-permute-start.2
  109.7 0.0 collective-permute-start.1
  110.3 5.7 %collective-permute-done.1 = f32[1]{0:T(128)} collective-permute-done((f32[1]{0:T(128)}, f32[1]{0:T(128)}, u32[]{:S(2)}, u32[]{:S(2)}) %collective-permute-start.1) | collective-permute-done | bytes 36 | tf_op jit(solution)/shard_map/ppermute | solution.py:11
  116.7 11.9 %collective-permute-start.3 = (f32[1]{0:T(128)}, f32[1]{0:T(128)}, u32[]{:S(2)}, u32[]{:S(2)}) collective-permute-start(f32[1]{0:T(128)} %select_n.19), channel_id=1, source_target_pairs={{0,2},{2,4},{4,6},{6,8},{8,10},{10,12},{12,14},{14,16},{16,18},{18... | collective-permute-start | bytes 20 | tf_op jit(solution)/shard_map/while/body/eval_jaxpr/ppermute | solution.py:11
  128.6 0.0 copy-done.1
  128.6 2.3 %fusion.6 = f32[256,256]{1,0:T(8,128)S(1)} fusion(f32[256,1024]{1,0:T(8,128)S(1)} %copy-done.1, f32[1,256,1024]{2,1,0:T(8,128)} %broadcast_select_fusion), kind=kOutput, calls=%fused_computation.7 | convolution fusion | flops 805306368 | bytes 2359296 | tf_op jit(solution)/shard_map/while/body/eval_jaxpr/xaq,ybq->xyab/dot_general | solution.py:16
  130.8 0.0 copy-start.3
  130.9 0.9 copy.6
  131.7 0.0 collective-permute-done.2
  131.7 3.0 %fusion.3 = f32[256,256]{1,0:T(8,128)} fusion(f32[256,1024]{1,0:T(8,128)S(1)} %copy-done.1, f32[1,256,1024]{2,1,0:T(8,128)} %collective-permute-done.2), kind=kOutput, calls=%fused_computation.4 | convolution fusion | flops 805306368 | bytes 2359296 | tf_op jit(solution)/shard_map/xaq,ybq->xyab/dot_general | solution.py:16
  134.7 0.0 copy-start.2
  134.7 1.1 copy.8
  135.8 0.0 collective-permute-done.3
  135.8 0.0 copy-done.3
  135.8 3.1 %fusion.1 = f32[256,1024]{1,0:T(8,128)S(1)} fusion(f32[1,256,1024]{2,1,0:T(8,128)} %collective-permute-done.2, f32[256,256]{1,0:T(8,128)} %fusion.3, f32[256,256]{0,1:T(8,128)S(1)} %copy.8, f32[]{:T(128)} %bitcast.17, f32[]{:T(128)} %bitcast.66, f32[256]{0:T(256)S(1)} %copy-done.3), kind=kOutput, calls=%fused_computation.2 | convolution fusion | flops 805699584 | bytes 2622472 | tf_op jit(solution)/shard_map/xyab,ybq->xaq/dot_general | solution.py:20
  138.9 0.0 copy-done.2
  138.9 3.3 %fusion = f32[1,256,1024]{2,1,0:T(8,128)} fusion(f32[256,1024]{1,0:T(8,128)S(1)} %fusion.1, f32[1,256,1024]{2,1,0:T(8,128)} %broadcast_select_fusion, f32[256,256]{1,0:T(8,128)S(1)} %fusion.6, f32[256,256]{0,1:T(8,128)S(1)} %copy-done.2, f32[]{:T(128)} %bitcast.11, f32[]{:T(128)} %bitcast.65, f32[256]{0:T(256)S(1)} %copy-done.3), kind=kOutput, calls=%fused_computation.1 | convolution fusion | flops 805961728 | bytes 3671048 | tf_op jit(solution)/shard_map/while/body/eval_jaxpr/xyab,ybq->xaq/dot_general | solution.py:20
  142.2 0.0 reduce-scatter.2.cloned.1.call-update
  142.3 17.1 %reduce-scatter.2.cloned.1.call-done = f32[1,256,512]{2,1,0:T(8,128)} async-done(((f32[1,256,1024]{2,1,0:T(8,128)}), f32[1,256,512]{2,1,0:T(8,128)}) %reduce-scatter.2.cloned.1.call-update) | async-done | bytes 524304 | tf_op jit(solution)/shard_map/reduce_scatter | solution.py:55
Async XLA Ops:
  6.5 1.6 copy-start
  6.5 46.9 %all-gather.4.cloned.1.call-start = ((), (), s32[]{:S(2)}) async-start(), calls=%async_computation.2 | async-start | bytes 1572864 | tf_op jit(solution)/shard_map/all_gather | solution.py:27
  32.5 47.0 %all-gather.6.cloned.1.call-start = ((), (), s32[]{:S(2)}) async-start(), calls=%async_computation.4 | async-start | bytes 1572864 | tf_op jit(solution)/shard_map/all_gather | solution.py:29
  58.1 101.3 %reduce-scatter.2.cloned.1.call-start = ((), (), s32[]{:S(2)}) async-start(), calls=%async_computation.3 | async-start | bytes 1572864 | tf_op jit(solution)/shard_map/reduce_scatter | solution.py:55
  79.5 49.1 %copy-start.1 = (f32[256,1024]{1,0:T(8,128)S(1)}, f32[256,1024]{1,0:T(8,128)}, u32[]{:S(2)}) copy-start(f32[256,1024]{1,0:T(8,128)} %all-gather.6.cloned.1.call-done) | copy-start | bytes 3145732
  79.5 27.7 %collective-permute-start = (f32[1,256,1024]{2,1,0:T(8,128)}, f32[1,256,1024]{2,1,0:T(8,128)}, u32[]{:S(2)}, u32[]{:S(2)}) collective-permute-start(f32[1,256,1024]{2,1,0:T(8,128)} %bitcast.67), channel_id=1, source_target_pairs={{0,4},{2,6},{4,8},{6,10},{8,12},{10,14},{12,16},{14,18},{16,20},{1... | collective-permute-start | bytes 3145736 | tf_op jit(solution)/shard_map/ppermute | solution.py:11
  109.7 22.1 %collective-permute-start.2 = (f32[1,256,1024]{2,1,0:T(8,128)}, f32[1,256,1024]{2,1,0:T(8,128)}, u32[]{:S(2)}, u32[]{:S(2)}) collective-permute-start(f32[1,256,1024]{2,1,0:T(8,128)} %broadcast_select_fusion), channel_id=1, source_target_pairs={{0,2},{2,4},{4,6},{6,8},{8,10},{10,12},{12,14},{14,16},{16,18},{18... | collective-permute-start | bytes 3145736 | tf_op jit(solution)/shard_map/while/body/eval_jaxpr/ppermute | solution.py:11
  109.7 6.4 %collective-permute-start.1 = (f32[1]{0:T(128)}, f32[1]{0:T(128)}, u32[]{:S(2)}, u32[]{:S(2)}) collective-permute-start(f32[1]{0:T(128)} %param.8), channel_id=1, source_target_pairs={{0,4},{2,6},{4,8},{6,10},{8,12},{10,14},{12,16},{14,18},{16,20},{1... | collective-permute-start | bytes 20 | tf_op jit(solution)/shard_map/ppermute | solution.py:11
  116.7 19.1 %collective-permute-start.3 = (f32[1]{0:T(128)}, f32[1]{0:T(128)}, u32[]{:S(2)}, u32[]{:S(2)}) collective-permute-start(f32[1]{0:T(128)} %select_n.19), channel_id=1, source_target_pairs={{0,2},{2,4},{4,6},{6,8},{8,10},{10,12},{12,14},{14,16},{16,18},{18... | collective-permute-start | bytes 20 | tf_op jit(solution)/shard_map/while/body/eval_jaxpr/ppermute | solution.py:11
  130.8 5.0 %copy-start.3 = (f32[256]{0:T(256)S(1)}, f32[256]{0:T(256)}, u32[]{:S(2)}) copy-start(f32[256]{0:T(256)} %param.9) | copy-start | bytes 3076
  134.7 4.2 %copy-start.2 = (f32[256,256]{0,1:T(8,128)S(1)}, f32[256,256]{0,1:T(8,128)}, u32[]{:S(2)}) copy-start(f32[256,256]{0,1:T(8,128)} %copy.6) | copy-start | bytes 786436
Sparse Core Ops, SparseCore 0:
  32.6 20.7 all-gather.3
  58.2 21.2 all-gather.5
  142.4 16.9 reduce-scatter.1
where the time goes:
time: 166 us
  waiting for transfers between devices  91.4 us (55%)
  blocking collectives  21.6 us (13%)
  matrix products  19 us (11%)
  between operations  14.6 us (9%)
  starting transfers between devices  13.4 us (8%)
  local copies, waits for them, and re-layouts  3.58 us (2%)
  other arithmetic  2.4 us (1%)
    ppermute x4, waiting for transfers between devices, from_behind(): return lax.ppermute(x, axis, [(i, (i + by) % count) for i in range(count)])  31.9 us
    all_to_all x1, blocking collectives, per_device(): lax.all_to_all(halfway, 'blk', split_axis=0, concat_axis=1, tiled=True)  21.6 us
    all_gather x1, waiting for transfers between devices, per_device(): fitted = lax.all_gather(fitted_part, 'rep', axis=2, tiled=True)  21.4 us
    all_gather x1, waiting for transfers between devices, per_device(): complete = lax.all_gather(regrouped, 'rep', axis=2, tiled=True)  20.9 us
    reduce_scatter x1, waiting for transfers between devices, per_device(): return lax.psum_scatter(gradient, 'rep', scatter_dimension=2, tiled=True)  17.1 us
    ppermute x4, starting transfers between devices, from_behind(): return lax.ppermute(x, axis, [(i, (i + by) % count) for i in range(count)])  13.3 us
    dot_general x2, matrix products, pair_terms(): jnp.einsum('xyab,ybq->xaq', amplitude, other_rows, precision=highest)  6.38 us
    dot_general x2, matrix products, pair_terms(): jnp.einsum('xaq,ybq->xyab', own_rows, other_rows, precision=highest)  5.22 us
  transfers between devices with their start and end apart: 7, of which 5 were waited for; matrix products, arithmetic and copies ran while one was open for 4% of the time, Pallas kernels for 0%

commit v1 on v0

--- a/solution.py
+++ b/solution.py
@@ -26,7 +26,16 @@
     regrouped = lax.all_to_all(halfway, "blk", split_axis=0, concat_axis=1, tiled=True)
     complete = lax.all_gather(regrouped, "rep", axis=2, tiled=True)
     fitted_part = jnp.einsum("xpa,pq->xaq", complete, metric_root, precision=highest)
-    fitted = lax.all_gather(fitted_part, "rep", axis=2, tiled=True)
+    u_next = lax.axis_size("rep")
+    everything = lax.axis_index("rep")
+    big, reached, passed = (u_next, everything, fitted_part.shape[2])
+    y1, value_now = (fitted_part, 1)
+    while value_now < big:
+        known = tuple(((src_i, (src_i - value_now) % big) for src_i in range(big)))
+        now = lax.ppermute(y1, "rep", known)
+        y1 = jnp.concatenate([y1, now], 2)
+        value_now = 2 * value_now
+    fitted = jnp.roll(y1, reached * passed, 2)
     replica = lax.axis_index("rep")
     replicas = lax.axis_size("rep")
     turns = TURNS

time: 166 us -> 158 us (0.952)
  waiting for transfers between devices: 91.4 us -> 83.1 us
    all_gather x1 -> x0, waiting for transfers between devices: 21.4 us -> none  [per_device(): fitted = lax.all_gather(fitted_part, 'rep', axis=2, tiled=True)]
    ppermute x0 -> x1, waiting for transfers between devices: none -> 12.9 us  [per_device(): now = lax.ppermute(y1, 'rep', known)]
  transfers between devices with their start and end apart: 7 -> 7, of which waited for: 5 -> 5; matrix products, arithmetic and copies ran while one was open for 4% -> 5% of each run, Pallas kernels for 0% -> 0%
where the time goes in v1:
time: 158 us
  waiting for transfers between devices  83.1 us (53%)
  blocking collectives  21.6 us (14%)
  matrix products  18.2 us (12%)
  between operations  14.7 us (9%)
  starting transfers between devices  13.7 us (9%)
  local copies, waits for them, and re-layouts  3.91 us (2%)
  other arithmetic  2.71 us (2%)
    ppermute x4, waiting for transfers between devices, from_behind(): return lax.ppermute(x, axis, [(i, (i + by) % count) for i in range(count)])  31 us
    all_to_all x1, blocking collectives, per_device(): lax.all_to_all(halfway, 'blk', split_axis=0, concat_axis=1, tiled=True)  21.6 us
    all_gather x1, waiting for transfers between devices, per_device(): complete = lax.all_gather(regrouped, 'rep', axis=2, tiled=True)  20.9 us
    reduce_scatter x1, waiting for transfers between devices, per_device(): return lax.psum_scatter(gradient, 'rep', scatter_dimension=2, tiled=True)  18.2 us
    ppermute x4, starting transfers between devices, from_behind(): return lax.ppermute(x, axis, [(i, (i + by) % count) for i in range(count)])  13.2 us
    ppermute x1, waiting for transfers between devices, per_device(): now = lax.ppermute(y1, 'rep', known)  12.9 us
    dot_general x2, matrix products, pair_terms(): jnp.einsum('xyab,ybq->xaq', amplitude, other_rows, precision=highest)  6.38 us
    dot_general x2, matrix products, pair_terms(): jnp.einsum('xaq,ybq->xyab', own_rows, other_rows, precision=highest)  5.22 us
  transfers between devices with their start and end apart: 7, of which 5 were waited for; matrix products, arithmetic and copies ran while one was open for 5% of the time, Pallas kernels for 0%

profile of v1, /device:TPU:0, one launch (start us, length us, event | category | flops | bytes accessed | tf_op | source)
XLA Modules:
  0.0 157.9 jit_solution(7391851413034033390)
XLA Ops:
  6.5 0.0 copy-start
  6.5 0.0 all-gather.2.cloned.1.call-start
  6.5 1.6 %copy-done = f32[16,64,512]{2,1,0:T(8,128)S(1)} copy-done((f32[16,64,512]{2,1,0:T(8,128)S(1)}, f32[16,64,512]{2,1,0:T(8,128)}, u32[]{:S(2)}) %copy-start) | copy-done | bytes 2097176
  8.1 2.7 %fusion.22 = f32[16,64,128]{2,1,0:T(8,128)S(1)} fusion(f32[16,64,512]{2,1,0:T(8,128)S(1)} %copy-done, f32[512,128]{1,0:T(8,128)} %param.6), kind=kOutput, calls=%fused_computation.29 | convolution fusion | flops 805306368 | bytes 2883584 | tf_op jit(solution)/shard_map/ipm,ma->ipa/dot_general | solution.py:25
  10.9 21.6 %all_to_all.12 = f32[16,64,128]{2,1,0:T(8,128)} all-to-all(f32[16,64,128]{2,1,0:T(8,128)S(1)} %fusion.22), channel_id=1, replica_groups=mesh['blk'=16,'rep'=2] {'blk'}, dimensions={0} | all-to-all | bytes 1048576 | tf_op jit(solution)/shard_map/all_to_all | solution.py:26
  32.5 0.0 all-gather.2.cloned.1.call-update
  32.5 0.0 reduce-scatter.2.cloned.1.call-start
  32.5 20.9 %all-gather.2.cloned.1.call-done = f32[1,1024,256]{2,1,0:T(8,128)} async-done(((f32[1,1024,128]{2,1,0:T(8,128)}), f32[1,1024,256]{2,1,0:T(8,128)}) %all-gather.2.cloned.1.call-update) | async-done | bytes 1048592 | tf_op jit(solution)/shard_map/all_gather | solution.py:27
  53.4 3.8 %convolution_bitcast_fusion = f32[1,256,512]{2,1,0:T(8,128)S(1)} fusion(f32[1024,512]{1,0:T(8,128)} %param.7, f32[1,1024,256]{2,1,0:T(8,128)} %all-gather.2.cloned.1.call-done), kind=kOutput, calls=%fused_computation.6 | convolution fusion | flops 1610612736 | bytes 3670016 | tf_op jit(solution)/shard_map/xpa,pq->xaq/dot_general | solution.py:28
  57.3 0.0 copy-start.1
  57.3 0.4 collective-permute-start
  57.7 0.4 copy-done.1
  58.1 12.9 %collective-permute-done = f32[1,256,512]{2,1,0:T(8,128)} collective-permute-done((f32[1,256,512]{2,1,0:T(8,128)S(1)}, f32[1,256,512]{2,1,0:T(8,128)}, u32[]{:S(2)}, u32[]{:S(2)}) %collective-permute-start) | collective-permute-done | bytes 524320 | tf_op jit(solution)/shard_map/ppermute | solution.py:35
  70.9 1.6 %fusion.3 = f32[1,256,1024]{2,1,0:T(8,128)S(1)} fusion(s32[]{:T(128)S(6)} %select_n.31, f32[1,256,512]{2,1,0:T(8,128)} %copy-done.1, f32[1,256,512]{2,1,0:T(8,128)} %collective-permute-done), kind=kLoop, calls=%fused_computation.9 | loop fusion | flops 786432 | bytes 2097156 | tf_op jit(solution)/shard_map/jit(_roll_dynamic)/concatenate | solution.py:38
  72.5 1.5 collective-permute-start.1
  74.1 25.2 %collective-permute-done.1 = f32[1,256,1024]{2,1,0:T(8,128)} collective-permute-done((f32[1,256,1024]{2,1,0:T(8,128)S(1)}, f32[1,256,1024]{2,1,0:T(8,128)}, u32[]{:S(2)}, u32[]{:S(2)}) %collective-permute-start.1) | collective-permute-done | bytes 1048608 | tf_op jit(solution)/shard_map/ppermute | solution.py:11
  99.3 1.1 broadcast_select_fusion
  100.4 0.0 collective-permute-start.3
  100.4 0.0 collective-permute-start.2
  101.1 5.8 %collective-permute-done.2 = f32[1]{0:T(128)} collective-permute-done((f32[1]{0:T(128)}, f32[1]{0:T(128)}, u32[]{:S(2)}, u32[]{:S(2)}) %collective-permute-start.2) | collective-permute-done | bytes 36 | tf_op jit(solution)/shard_map/ppermute | solution.py:11
  107.5 11.7 %collective-permute-start.4 = (f32[1]{0:T(128)}, f32[1]{0:T(128)}, u32[]{:S(2)}, u32[]{:S(2)}) collective-permute-start(f32[1]{0:T(128)} %select_n.34), channel_id=1, source_target_pairs={{0,2},{2,4},{4,6},{6,8},{8,10},{10,12},{12,14},{14,16},{16,18},{18... | collective-permute-start | bytes 20 | tf_op jit(solution)/shard_map/while/body/eval_jaxpr/ppermute | solution.py:11
  119.2 2.3 %fusion.9 = f32[256,256]{1,0:T(8,128)S(1)} fusion(f32[1,256,1024]{2,1,0:T(8,128)S(1)} %fusion.3, f32[1,256,1024]{2,1,0:T(8,128)} %broadcast_select_fusion), kind=kOutput, calls=%fused_computation.15 | convolution fusion | flops 805306368 | bytes 2359296 | tf_op jit(solution)/shard_map/while/body/eval_jaxpr/xaq,ybq->xyab/dot_general | solution.py:16
  121.4 0.0 copy-start.3
  121.4 0.8 copy.6
  122.3 0.0 collective-permute-done.3
  122.3 3.0 %fusion.6 = f32[256,256]{1,0:T(8,128)} fusion(f32[1,256,1024]{2,1,0:T(8,128)} %collective-permute-done.3, f32[1,256,1024]{2,1,0:T(8,128)S(1)} %fusion.3), kind=kOutput, calls=%fused_computation.12 | convolution fusion | flops 805306368 | bytes 2359296 | tf_op jit(solution)/shard_map/xaq,ybq->xyab/dot_general | solution.py:16
  125.2 0.0 copy-start.2
  125.2 1.1 copy.8
  126.4 0.0 collective-permute-done.4
  126.4 0.0 copy-done.3
  126.4 3.1 %fusion.4 = f32[256,1024]{1,0:T(8,128)S(1)} fusion(f32[1,256,1024]{2,1,0:T(8,128)} %collective-permute-done.3, f32[256,256]{1,0:T(8,128)} %fusion.6, f32[256,256]{0,1:T(8,128)S(1)} %copy.8, f32[]{:T(128)} %bitcast.18, f32[]{:T(128)} %bitcast.69, f32[256]{0:T(256)S(1)} %copy-done.3), kind=kOutput, calls=%fused_computation.10 | convolution fusion | flops 805699584 | bytes 2622472 | tf_op jit(solution)/shard_map/xyab,ybq->xaq/dot_general | solution.py:20
  129.5 0.0 copy-done.2
  129.5 3.3 %fusion = f32[1,256,1024]{2,1,0:T(8,128)} fusion(f32[256,1024]{1,0:T(8,128)S(1)} %fusion.4, f32[1,256,1024]{2,1,0:T(8,128)} %broadcast_select_fusion, f32[256,256]{1,0:T(8,128)S(1)} %fusion.9, f32[256,256]{0,1:T(8,128)S(1)} %copy-done.2, f32[]{:T(128)} %bitcast.12, f32[]{:T(128)} %bitcast.68, f32[256]{0:T(256)S(1)} %copy-done.3), kind=kOutput, calls=%fused_computation.5 | convolution fusion | flops 805961728 | bytes 3671048 | tf_op jit(solution)/shard_map/while/body/eval_jaxpr/xyab,ybq->xaq/dot_general | solution.py:20
  132.8 0.0 reduce-scatter.2.cloned.1.call-update
  132.8 18.2 %reduce-scatter.2.cloned.1.call-done = f32[1,256,512]{2,1,0:T(8,128)} async-done(((f32[1,256,1024]{2,1,0:T(8,128)}), f32[1,256,512]{2,1,0:T(8,128)}) %reduce-scatter.2.cloned.1.call-update) | async-done | bytes 524304 | tf_op jit(solution)/shard_map/reduce_scatter | solution.py:64
Async XLA Ops:
  6.5 1.6 %copy-start = (f32[16,64,512]{2,1,0:T(8,128)S(1)}, f32[16,64,512]{2,1,0:T(8,128)}, u32[]{:S(2)}) copy-start(f32[16,64,512]{2,1,0:T(8,128)} %param.5) | copy-start | bytes 6291460
  6.5 46.9 %all-gather.2.cloned.1.call-start = ((), (), s32[]{:S(2)}) async-start(), calls=%async_computation.2 | async-start | bytes 1572864 | tf_op jit(solution)/shard_map/all_gather | solution.py:27
  32.5 118.6 %reduce-scatter.2.cloned.1.call-start = ((), (), s32[]{:S(2)}) async-start(), calls=%async_computation.3 | async-start | bytes 1572864 | tf_op jit(solution)/shard_map/reduce_scatter | solution.py:64
  57.3 0.8 copy-start.1
  57.3 13.7 %collective-permute-start = (f32[1,256,512]{2,1,0:T(8,128)S(1)}, f32[1,256,512]{2,1,0:T(8,128)}, u32[]{:S(2)}, u32[]{:S(2)}) collective-permute-start(f32[1,256,512]{2,1,0:T(8,128)S(1)} %convolution_bitcast_fusion), channel_id=1, source_target_pairs={{0,1},{1,0},{2,3},{3,2},{4,5},{5,4},{6,7},{7,6},{8,9},{9,8},{10,11... | collective-permute-start | bytes 1572872 | tf_op jit(solution)/shard_map/ppermute | solution.py:35
  72.5 26.7 %collective-permute-start.1 = (f32[1,256,1024]{2,1,0:T(8,128)S(1)}, f32[1,256,1024]{2,1,0:T(8,128)}, u32[]{:S(2)}, u32[]{:S(2)}) collective-permute-start(f32[1,256,1024]{2,1,0:T(8,128)S(1)} %fusion.3), channel_id=1, source_target_pairs={{0,4},{2,6},{4,8},{6,10},{8,12},{10,14},{12,16},{14,18},{16,20},{1... | collective-permute-start | bytes 3145736 | tf_op jit(solution)/shard_map/ppermute | solution.py:11
  100.4 21.9 %collective-permute-start.3 = (f32[1,256,1024]{2,1,0:T(8,128)}, f32[1,256,1024]{2,1,0:T(8,128)}, u32[]{:S(2)}, u32[]{:S(2)}) collective-permute-start(f32[1,256,1024]{2,1,0:T(8,128)} %broadcast_select_fusion), channel_id=1, source_target_pairs={{0,2},{2,4},{4,6},{6,8},{8,10},{10,12},{12,14},{14,16},{16,18},{18... | collective-permute-start | bytes 3145736 | tf_op jit(solution)/shard_map/while/body/eval_jaxpr/ppermute | solution.py:11
  100.4 6.5 %collective-permute-start.2 = (f32[1]{0:T(128)}, f32[1]{0:T(128)}, u32[]{:S(2)}, u32[]{:S(2)}) collective-permute-start(f32[1]{0:T(128)} %param.8), channel_id=1, source_target_pairs={{0,4},{2,6},{4,8},{6,10},{8,12},{10,14},{12,16},{14,18},{16,20},{1... | collective-permute-start | bytes 20 | tf_op jit(solution)/shard_map/ppermute | solution.py:11
  107.5 18.9 %collective-permute-start.4 = (f32[1]{0:T(128)}, f32[1]{0:T(128)}, u32[]{:S(2)}, u32[]{:S(2)}) collective-permute-start(f32[1]{0:T(128)} %select_n.34), channel_id=1, source_target_pairs={{0,2},{2,4},{4,6},{6,8},{8,10},{10,12},{12,14},{14,16},{16,18},{18... | collective-permute-start | bytes 20 | tf_op jit(solution)/shard_map/while/body/eval_jaxpr/ppermute | solution.py:11
  121.4 4.9 %copy-start.3 = (f32[256]{0:T(256)S(1)}, f32[256]{0:T(256)}, u32[]{:S(2)}) copy-start(f32[256]{0:T(256)} %param.9) | copy-start | bytes 3076
  125.2 4.2 %copy-start.2 = (f32[256,256]{0,1:T(8,128)S(1)}, f32[256,256]{0,1:T(8,128)}, u32[]{:S(2)}) copy-start(f32[256,256]{0,1:T(8,128)} %copy.6) | copy-start | bytes 786436
Sparse Core Ops, SparseCore 0:
  32.6 20.7 all-gather.1
  132.9 18.0 reduce-scatter.1
